TPU v7x, 32 devices: a whole 2x2x4 slice. The times are simulated.
32 devices in a mesh: groups: 2 (over y), row: 4 (over z), col: 2 (over x), rep: 2 (over core).
Axes of the slice: x: 2, y: 2, z: 4, core: 2. Of those that a mesh axis runs over, the one named last changes fastest.
Arguments:
- kernel: float32 [32768, 16384], P(('groups', 'row'), ('col', 'rep')), parts along dimension 0, may hold values from 0 to 2, as said below
- source: float32 [64, 16384], P('groups', 'row'), parts along dimension 0, may hold values from 0.5 to 2, as said below
- target: float32 [64, 16384], P('groups', ('col', 'rep')), parts along dimension 0, may hold values from 0.5 to 2, as said below
Outputs:
- left_scale: float32 [64, 16384], P('groups', 'row'), parts along dimension 0
- right_scale: float32 [64, 16384], P('groups', ('col', 'rep')), parts along dimension 0
- errors: float32 [6, 32], P('groups'), parts along dimension 0
There are 2 independent parts, one for each index of `groups`. A program takes and returns all parts, laid end to end along the dimension named above; each array names one. Nothing has to cross between parts.
Inputs may be any that keep to these rules, and one draw needn't show every extreme that they name: `kernel`: every entry is positive. `source`: every entry is positive. `target`: every entry is positive.
All inputs are finite; a program needn't handle non-finite values.
Results may differ from a plain program's by a relative error of at most 0.0001.
Values sent between devices are 32-bit elements; how exact they have to be, the bound alone decides.
A program may use at most 128 MiB of HBM per device.

v0:
```python
import jax
import jax.numpy as jnp
from jax import lax
from jax.sharding import PartitionSpec as P

N = 16384
ITERS = 3


def local(kernel, source, target):
    columns = kernel.shape[1]
    right_scale = jnp.ones(target.shape, jnp.float32)
    left_scale = source
    share = columns // lax.axis_size("row")
    offset = lax.axis_index("row") * share
    errors = []
    for step in range(ITERS):
        partial_value = lax.dot_general(
            right_scale, kernel, (((1,), (1,)), ((), ())), precision=lax.Precision.HIGHEST
        )
        left_scale = source / lax.psum(partial_value, ("col", "rep"))
        back = jnp.dot(left_scale, kernel, precision=lax.Precision.HIGHEST)
        old_piece = lax.dynamic_slice_in_dim(right_scale, offset, share, 1)
        target_piece = lax.dynamic_slice_in_dim(target, offset, share, 1)
        total_piece = lax.psum_scatter(back, "row", scatter_dimension=1, tiled=True)
        right_scale = lax.all_gather(target_piece / total_piece, "row", axis=1, tiled=True)
        term = jnp.sum(jnp.abs(old_piece * total_piece - target_piece), axis=1) / N
        errors.append(lax.psum(term, ("row", "col", "rep")))
    stacked = jnp.stack(errors)
    return (left_scale, right_scale, stacked)


def solution(mesh):
    return jax.shard_map(
        local,
        mesh=mesh,
        in_specs=(
            P(("groups", "row"), ("col", "rep")),
            P("groups", "row"),
            P("groups", ("col", "rep")),
        ),
        out_specs=(P("groups", "row"), P("groups", ("col", "rep")), P("groups", None)),
        check_vma=False,
    )
```

profile of v0, /device:TPU:0, one launch (start us, length us, event | category | flops | bytes accessed | tf_op | source)
XLA Modules:
  0.0 597.1 jit_solution(12538912805392526422)
XLA Ops:
  7.2 0.0 copy-start
  7.2 0.0 all-reduce.5.cloned.1.call-start
  7.2 66.4 %fusion.4 = f32[32,4096]{1,0:T(8,128)} fusion(f32[4096,4096]{1,0:T(8,128)} %param.3), kind=kOutput, calls=%fused_computation.4 | convolution fusion | flops 6442450944 | bytes 67633152 | tf_op jit(solution)/shard_map/dot_general | solution.py:18
  73.7 0.0 copy-start.4
  73.7 0.0 all-reduce.5.cloned.1.call-update
  73.7 0.3 reduce-scatter.4.cloned.1.call-start
  74.0 36.0 %all-reduce.5.cloned.1.call-done = f32[32,4096]{1,0:T(8,128)} async-done(((f32[32,4096]{1,0:T(8,128)}), f32[32,4096]{1,0:T(8,128)}) %all-reduce.5.cloned.1.call-update) | async-done | bytes 524304 | tf_op jit(solution)/shard_map/psum | solution.py:21
  110.0 0.0 copy-done
  110.0 44.8 %fusion.2 = f32[32,4096]{1,0:T(8,128)} fusion(f32[4096,4096]{1,0:T(8,128)} %param.3, f32[32,4096]{1,0:T(8,128)S(1)} %copy-done, f32[32,4096]{1,0:T(8,128)} %all-reduce.5.cloned.1.call-done), kind=kOutput, calls=%fused_computation.2 | convolution fusion | flops 6442582016 | bytes 68681728 | tf_op jit(solution)/shard_map/dot_general | solution.py:22
  154.8 0.0 reduce-scatter.4.cloned.1.call-update
  154.9 0.0 all-reduce.7.cloned.1.call-start
  154.9 22.1 %reduce-scatter.4.cloned.1.call-done = f32[32,1024]{1,0:T(8,128)} async-done(((f32[32,4096]{1,0:T(8,128)}), f32[32,1024]{1,0:T(8,128)}) %reduce-scatter.4.cloned.1.call-update) | async-done | bytes 131088 | tf_op jit(solution)/shard_map/reduce_scatter | solution.py:25
  177.0 0.0 copy-done.4
  177.0 0.9 dynamic-slice_divide_fusion.2
  177.9 15.7 %all_gather.9 = f32[32,4096]{1,0:T(8,128)S(1)} all-gather(f32[32,1024]{1,0:T(8,128)S(1)} %dynamic-slice_divide_fusion.2), channel_id=1, replica_groups=mesh['groups'=2,'row'=4,'col'=2,'rep'=2] {'row'}, dimensions={1}, use_global_device_ids=true | all-gather | bytes 655360 | tf_op jit(solution)/shard_map/all_gather | solution.py:26
  193.7 66.5 %fusion.7 = f32[32,4096]{1,0:T(8,128)} fusion(f32[32,4096]{1,0:T(8,128)S(1)} %all_gather.9, f32[4096,4096]{1,0:T(8,128)} %param.3), kind=kOutput, calls=%fused_computation.17 | convolution fusion | flops 6442450944 | bytes 68157440 | tf_op jit(solution)/shard_map/dot_general | solution.py:18
  260.2 0.0 all-reduce.7.cloned.1.call-update
  260.2 0.2 reduce-scatter.6.cloned.1.call-start
  260.4 31.8 %all-reduce.7.cloned.1.call-done = f32[32,4096]{1,0:T(8,128)} async-done(((f32[32,4096]{1,0:T(8,128)}), f32[32,4096]{1,0:T(8,128)}) %all-reduce.7.cloned.1.call-update) | async-done | bytes 524304 | tf_op jit(solution)/shard_map/psum | solution.py:21
  292.2 44.8 %fusion = f32[32,4096]{1,0:T(8,128)} fusion(f32[4096,4096]{1,0:T(8,128)} %param.3, f32[32,4096]{1,0:T(8,128)S(1)} %copy-done, f32[32,4096]{1,0:T(8,128)} %all-reduce.7.cloned.1.call-done), kind=kOutput, calls=%fused_computation | convolution fusion | flops 6442582016 | bytes 68681728 | tf_op jit(solution)/shard_map/dot_general | solution.py:22
  337.0 0.0 reduce-scatter.6.cloned.1.call-update
  337.0 0.0 all-reduce.9.cloned.1.call-start
  337.1 22.0 %reduce-scatter.6.cloned.1.call-done = f32[32,1024]{1,0:T(8,128)} async-done(((f32[32,4096]{1,0:T(8,128)}), f32[32,1024]{1,0:T(8,128)}) %reduce-scatter.6.cloned.1.call-update) | async-done | bytes 131088 | tf_op jit(solution)/shard_map/reduce_scatter | solution.py:25
  359.1 0.9 dynamic-slice_divide_fusion.1
  360.0 15.7 %all_gather.10 = f32[32,4096]{1,0:T(8,128)S(1)} all-gather(f32[32,1024]{1,0:T(8,128)S(1)} %dynamic-slice_divide_fusion.1), channel_id=1, replica_groups=mesh['groups'=2,'row'=4,'col'=2,'rep'=2] {'row'}, dimensions={1}, use_global_device_ids=true | all-gather | bytes 655360 | tf_op jit(solution)/shard_map/all_gather | solution.py:26
  375.7 66.5 %fusion.8 = f32[32,4096]{1,0:T(8,128)} fusion(f32[32,4096]{1,0:T(8,128)S(1)} %all_gather.10, f32[4096,4096]{1,0:T(8,128)} %param.3), kind=kOutput, calls=%fused_computation.18 | convolution fusion | flops 6442450944 | bytes 68157440 | tf_op jit(solution)/shard_map/dot_general | solution.py:18
  442.2 0.0 copy-start.2
  442.2 0.0 copy-start.3
  442.2 0.0 all-reduce.9.cloned.1.call-update
  442.2 0.3 reduce-scatter.8.cloned.1.call-start
  442.5 31.6 %all-reduce.9.cloned.1.call-done = f32[32,4096]{1,0:T(8,128)} async-done(((f32[32,4096]{1,0:T(8,128)}), f32[32,4096]{1,0:T(8,128)}) %all-reduce.9.cloned.1.call-update) | async-done | bytes 524304 | tf_op jit(solution)/shard_map/psum | solution.py:21
  474.2 1.1 div.31
  475.3 0.0 copy-start.1
  475.3 45.0 %fusion.9 = f32[32,4096]{1,0:T(8,128)} fusion(f32[32,4096]{1,0:T(8,128)S(1)} %div.31, f32[4096,4096]{1,0:T(8,128)} %param.3), kind=kOutput, calls=%fused_computation.19 | convolution fusion | flops 6442450944 | bytes 68157440 | tf_op jit(solution)/shard_map/dot_general | solution.py:22
  520.3 0.0 reduce-scatter.8.cloned.1.call-update
  520.4 22.1 %reduce-scatter.8.cloned.1.call-done = f32[32,1024]{1,0:T(8,128)} async-done(((f32[32,4096]{1,0:T(8,128)}), f32[32,1024]{1,0:T(8,128)}) %reduce-scatter.8.cloned.1.call-update) | async-done | bytes 131088 | tf_op jit(solution)/shard_map/reduce_scatter | solution.py:25
  542.5 0.0 copy-done.2
  542.5 0.0 copy-done.3
  542.5 1.1 abs_reduce_fusion.2
  543.6 15.3 %all_gather.11 = f32[32,4096]{1,0:T(8,128)S(1)} all-gather(f32[32,1024]{1,0:T(8,128)S(1)} %get-tuple-element.9), channel_id=1, replica_groups=mesh['groups'=2,'row'=4,'col'=2,'rep'=2] {'row'}, dimensions={1}, use_global_device_ids=true | all-gather | bytes 655360 | tf_op jit(solution)/shard_map/all_gather | solution.py:26
  558.9 29.5 %all-reduce = (f32[1,32]{1,0:T(1,128)S(1)}, f32[1,32]{1,0:T(1,128)S(1)}, f32[1,32]{1,0:T(1,128)S(1)}) all-reduce(f32[1,32]{1,0:T(1,128)S(1)} %get-tuple-element.10, f32[1,32]{1,0:T(1,128)S(1)} %get-tuple-element.11, f32[1,32]{1,0:T(1,128)S(1)} %multiply_bitcast_fusion.2), channel_id=1, replica_groups=mesh['groups'=2,'row'=4,'col'=2,'rep'=2] {'row','col','rep'}, use_global_device_ids=true, to_apply=%region_11.0 | all-reduce | flops 96 | bytes 768 | tf_op jit(solution)/shard_map/psum | solution.py:28
  588.4 0.6 pad_maximum_fusion
  589.0 0.8 copy.10
  589.8 0.0 copy-done.1
  (2 shorter events, 0.0 us)
Async XLA Ops:
  7.2 102.8 %copy-start = (f32[32,4096]{1,0:T(8,128)S(1)}, f32[32,4096]{1,0:T(8,128)}, u32[]{:S(2)}) copy-start(f32[32,4096]{1,0:T(8,128)} %param.4) | copy-start | bytes 1572868
  7.2 102.8 %all-reduce.5.cloned.1.call-start = ((), (), s32[]{:S(2)}) async-start(), calls=%async_computation.3 | async-start | bytes 1048576 | tf_op jit(solution)/shard_map/psum | solution.py:21
  73.7 103.3 %copy-start.4 = (f32[32,4096]{1,0:T(8,128)S(1)}, f32[32,4096]{1,0:T(8,128)}, u32[]{:S(2)}) copy-start(f32[32,4096]{1,0:T(8,128)} %param.5) | copy-start | bytes 1572868
  73.7 103.3 %reduce-scatter.4.cloned.1.call-start = ((), (), s32[]{:S(2)}) async-start(), calls=%async_computation.4 | async-start | bytes 655360 | tf_op jit(solution)/shard_map/reduce_scatter | solution.py:25
  154.9 137.3 %all-reduce.7.cloned.1.call-start = ((), (), s32[]{:S(2)}) async-start(), calls=%async_computation.5 | async-start | bytes 1048576 | tf_op jit(solution)/shard_map/psum | solution.py:21
  260.2 98.9 %reduce-scatter.6.cloned.1.call-start = ((), (), s32[]{:S(2)}) async-start(), calls=%async_computation.6 | async-start | bytes 655360 | tf_op jit(solution)/shard_map/reduce_scatter | solution.py:25
  337.0 137.1 %all-reduce.9.cloned.1.call-start = ((), (), s32[]{:S(2)}) async-start(), calls=%async_computation.7 | async-start | bytes 1048576 | tf_op jit(solution)/shard_map/psum | solution.py:21
  442.2 100.3 %copy-start.2 = (f32[32,1024]{1,0:T(8,128)S(1)}, f32[32,1024]{1,0:T(8,128)}, u32[]{:S(2)}) copy-start(f32[32,1024]{1,0:T(8,128)} %reduce-scatter.4.cloned.1.call-done) | copy-start | bytes 393220
  442.2 100.3 %copy-start.3 = (f32[32,1024]{1,0:T(8,128)S(1)}, f32[32,1024]{1,0:T(8,128)}, u32[]{:S(2)}) copy-start(f32[32,1024]{1,0:T(8,128)} %reduce-scatter.6.cloned.1.call-done) | copy-start | bytes 393220
  442.2 100.2 %reduce-scatter.8.cloned.1.call-start = ((), (), s32[]{:S(2)}) async-start(), calls=%async_computation.8 | async-start | bytes 655360 | tf_op jit(solution)/shard_map/reduce_scatter | solution.py:25
  475.3 114.5 %copy-start.1 = (f32[32,4096]{1,0:T(8,128)}, f32[32,4096]{1,0:T(8,128)S(1)}, u32[]{:S(2)}) copy-start(f32[32,4096]{1,0:T(8,128)S(1)} %div.31) | copy-start | bytes 1572868
Sparse Core Ops, SparseCore 0:
  73.8 36.1 all-reduce.4
  155.0 21.9 reduce-scatter.3
  260.3 31.8 all-reduce.6
  337.1 21.9 reduce-scatter.5
  442.4 31.7 all-reduce.8
  520.5 21.9 reduce-scatter.7
where the time goes:
time: 606 us; the launch traced here: 597 us
  matrix products  334 us (55%)
  waiting for transfers between devices  166 us (27%)
  blocking collectives  76.2 us (13%)
  between operations  14.6 us (2%)
    dot_general x3, matrix products, local(): lax.dot_general(right_scale, kernel, (((1,), (1,)), ((), ())), precision=...  199 us
    dot_general x3, matrix products, local(): back = jnp.dot(left_scale, kernel, precision=lax.Precision.HIGHEST)  135 us
    psum x3, waiting for transfers between devices, local(): left_scale = source / lax.psum(partial_value, ('col', 'rep'))  99.4 us
    reduce_scatter x3, waiting for transfers between devices, local(): total_piece = lax.psum_scatter(back, 'row', scatter_dimension=1, tiled=True)  66.2 us
    all_gather x3, blocking collectives, local(): lax.all_gather(target_piece / total_piece, 'row', axis=1, tiled=True)  46.8 us
    psum x1, blocking collectives, local(): errors.append(lax.psum(term, ('row', 'col', 'rep')))  29.5 us
  transfers between devices with their start and end apart: 6, of which 6 were waited for; matrix products, arithmetic and copies ran while one was open for 0% of the time, Pallas kernels for 0%

commit v1 on v0

--- a/solution.py
+++ b/solution.py
@@ -23,7 +23,7 @@
         old_piece = lax.dynamic_slice_in_dim(right_scale, offset, share, 1)
         target_piece = lax.dynamic_slice_in_dim(target, offset, share, 1)
         total_piece = lax.psum_scatter(back, "row", scatter_dimension=1, tiled=True)
-        right_scale = lax.all_gather(target_piece / total_piece, "row", axis=1, tiled=True)
+        right_scale = jnp.concatenate(lax.all_gather(target_piece / total_piece, "row"), axis=1)
         term = jnp.sum(jnp.abs(old_piece * total_piece - target_piece), axis=1) / N
         errors.append(lax.psum(term, ("row", "col", "rep")))
     stacked = jnp.stack(errors)

time: 606 us -> 607 us (level)
  no operation moved by 1% of the time
where the time goes in v1:
time: 607 us; the launch traced here: 599 us
  matrix products  335 us (55%)
  waiting for transfers between devices  166 us (27%)
  blocking collectives  75.5 us (12%)
  between operations  14.6 us (2%)
    dot_general x3, matrix products, local(): lax.dot_general(right_scale, kernel, (((1,), (1,)), ((), ())), precision=...  200 us
    dot_general x3, matrix products, local(): back = jnp.dot(left_scale, kernel, precision=lax.Precision.HIGHEST)  135 us
    psum x3, waiting for transfers between devices, local(): left_scale = source / lax.psum(partial_value, ('col', 'rep'))  99.9 us
    reduce_scatter x3, waiting for transfers between devices, local(): total_piece = lax.psum_scatter(back, 'row', scatter_dimension=1, tiled=True)  66.2 us
    all_gather x3, blocking collectives, local(): lax.all_gather(target_piece / total_piece, 'row')  46 us
    psum x1, blocking collectives, local(): errors.append(lax.psum(term, ('row', 'col', 'rep')))  29.5 us
  transfers between devices with their start and end apart: 6, of which 6 were waited for; matrix products, arithmetic and copies ran while one was open for 0% of the time, Pallas kernels for 0%

profile of v1, /device:TPU:0, one launch (start us, length us, event | category | flops | bytes accessed | tf_op | source)
XLA Modules:
  0.0 598.6 jit_solution(3108128837993985100)
XLA Ops:
  7.2 0.0 copy-start
  7.2 0.0 all-reduce.5.cloned.1.call-start
  7.2 66.4 %fusion.4 = f32[32,4096]{1,0:T(8,128)} fusion(f32[4096,4096]{1,0:T(8,128)} %param.3), kind=kOutput, calls=%fused_computation.4 | convolution fusion | flops 6442450944 | bytes 67633152 | tf_op jit(solution)/shard_map/dot_general | solution.py:18
  73.7 0.0 copy-start.4
  73.7 0.0 all-reduce.5.cloned.1.call-update
  73.7 0.3 reduce-scatter.4.cloned.1.call-start
  74.0 36.0 %all-reduce.5.cloned.1.call-done = f32[32,4096]{1,0:T(8,128)} async-done(((f32[32,4096]{1,0:T(8,128)}), f32[32,4096]{1,0:T(8,128)}) %all-reduce.5.cloned.1.call-update) | async-done | bytes 524304 | tf_op jit(solution)/shard_map/psum | solution.py:21
  110.0 0.0 copy-done
  110.0 44.8 %fusion.2 = f32[32,4096]{1,0:T(8,128)} fusion(f32[4096,4096]{1,0:T(8,128)} %param.3, f32[32,4096]{1,0:T(8,128)S(1)} %copy-done, f32[32,4096]{1,0:T(8,128)} %all-reduce.5.cloned.1.call-done), kind=kOutput, calls=%fused_computation.2 | convolution fusion | flops 6442582016 | bytes 68681728 | tf_op jit(solution)/shard_map/dot_general | solution.py:22
  154.8 0.0 reduce-scatter.4.cloned.1.call-update
  154.9 0.0 all-reduce.7.cloned.1.call-start
  154.9 22.1 %reduce-scatter.4.cloned.1.call-done = f32[32,1024]{1,0:T(8,128)} async-done(((f32[32,4096]{1,0:T(8,128)}), f32[32,1024]{1,0:T(8,128)}) %reduce-scatter.4.cloned.1.call-update) | async-done | bytes 131088 | tf_op jit(solution)/shard_map/reduce_scatter | solution.py:25
  177.0 0.0 copy-done.4
  177.0 0.9 dynamic-slice_divide_fusion.2
  177.9 15.3 %all-gather = f32[128,1024]{1,0:T(8,128)S(1)} all-gather(f32[32,1024]{1,0:T(8,128)S(1)} %dynamic-slice_divide_fusion.2), channel_id=2, replica_groups=mesh['groups'=2,'row'=4,'col'=2,'rep'=2] {'row'}, dimensions={0}, use_global_device_ids=true | all-gather | bytes 655360 | tf_op jit(solution)/shard_map/all_gather | solution.py:26
  193.3 0.3 copy.6
  193.6 0.3 copy.10
  193.9 66.9 %fusion.7 = f32[32,4096]{1,0:T(8,128)} fusion(f32[32,4096]{1,0:T(8,128)S(1)} %bitcast.28, f32[4096,4096]{1,0:T(8,128)} %param.3), kind=kOutput, calls=%fused_computation.17 | convolution fusion | flops 6442450944 | bytes 68157440 | tf_op jit(solution)/shard_map/dot_general | solution.py:18
  260.8 0.0 all-reduce.7.cloned.1.call-update
  260.9 0.0 reduce-scatter.6.cloned.1.call-start
  260.9 31.9 %all-reduce.7.cloned.1.call-done = f32[32,4096]{1,0:T(8,128)} async-done(((f32[32,4096]{1,0:T(8,128)}), f32[32,4096]{1,0:T(8,128)}) %all-reduce.7.cloned.1.call-update) | async-done | bytes 524304 | tf_op jit(solution)/shard_map/psum | solution.py:21
  292.8 45.0 %fusion = f32[32,4096]{1,0:T(8,128)} fusion(f32[4096,4096]{1,0:T(8,128)} %param.3, f32[32,4096]{1,0:T(8,128)S(1)} %copy-done, f32[32,4096]{1,0:T(8,128)} %all-reduce.7.cloned.1.call-done), kind=kOutput, calls=%fused_computation | convolution fusion | flops 6442582016 | bytes 68681728 | tf_op jit(solution)/shard_map/dot_general | solution.py:22
  337.8 0.0 reduce-scatter.6.cloned.1.call-update
  337.9 0.0 all-reduce.9.cloned.1.call-start
  337.9 22.1 %reduce-scatter.6.cloned.1.call-done = f32[32,1024]{1,0:T(8,128)} async-done(((f32[32,4096]{1,0:T(8,128)}), f32[32,1024]{1,0:T(8,128)}) %reduce-scatter.6.cloned.1.call-update) | async-done | bytes 131088 | tf_op jit(solution)/shard_map/reduce_scatter | solution.py:25
  360.0 0.9 dynamic-slice_divide_fusion.1
  360.9 15.3 %all-gather.1 = f32[128,1024]{1,0:T(8,128)S(1)} all-gather(f32[32,1024]{1,0:T(8,128)S(1)} %dynamic-slice_divide_fusion.1), channel_id=3, replica_groups=mesh['groups'=2,'row'=4,'col'=2,'rep'=2] {'row'}, dimensions={0}, use_global_device_ids=true | all-gather | bytes 655360 | tf_op jit(solution)/shard_map/all_gather | solution.py:26
  376.2 0.3 copy.7
  376.6 0.3 copy.11
  376.9 66.7 %fusion.8 = f32[32,4096]{1,0:T(8,128)} fusion(f32[32,4096]{1,0:T(8,128)S(1)} %bitcast.30, f32[4096,4096]{1,0:T(8,128)} %param.3), kind=kOutput, calls=%fused_computation.18 | convolution fusion | flops 6442450944 | bytes 68157440 | tf_op jit(solution)/shard_map/dot_general | solution.py:18
  443.6 0.0 copy-start.2
  443.6 0.0 copy-start.3
  443.6 0.0 all-reduce.9.cloned.1.call-update
  443.6 0.0 reduce-scatter.8.cloned.1.call-start
  443.7 31.9 %all-reduce.9.cloned.1.call-done = f32[32,4096]{1,0:T(8,128)} async-done(((f32[32,4096]{1,0:T(8,128)}), f32[32,4096]{1,0:T(8,128)}) %all-reduce.9.cloned.1.call-update) | async-done | bytes 524304 | tf_op jit(solution)/shard_map/psum | solution.py:21
  475.6 1.1 div.31
  476.7 0.0 copy-start.1
  476.8 45.1 %fusion.9 = f32[32,4096]{1,0:T(8,128)} fusion(f32[32,4096]{1,0:T(8,128)S(1)} %div.31, f32[4096,4096]{1,0:T(8,128)} %param.3), kind=kOutput, calls=%fused_computation.19 | convolution fusion | flops 6442450944 | bytes 68157440 | tf_op jit(solution)/shard_map/dot_general | solution.py:22
  521.9 0.0 reduce-scatter.8.cloned.1.call-update
  521.9 22.1 %reduce-scatter.8.cloned.1.call-done = f32[32,1024]{1,0:T(8,128)} async-done(((f32[32,4096]{1,0:T(8,128)}), f32[32,1024]{1,0:T(8,128)}) %reduce-scatter.8.cloned.1.call-update) | async-done | bytes 131088 | tf_op jit(solution)/shard_map/reduce_scatter | solution.py:25
  544.0 0.0 copy-done.2
  544.0 0.0 copy-done.3
  544.0 1.1 abs_reduce_fusion.2
  545.1 15.3 %all-gather.2 = f32[128,1024]{1,0:T(8,128)S(1)} all-gather(f32[32,1024]{1,0:T(8,128)S(1)} %get-tuple-element.9), channel_id=4, replica_groups=mesh['groups'=2,'row'=4,'col'=2,'rep'=2] {'row'}, dimensions={0}, use_global_device_ids=true | all-gather | bytes 655360 | tf_op jit(solution)/shard_map/all_gather | solution.py:26
  560.5 0.8 copy.9
  561.3 29.5 %all-reduce = (f32[1,32]{1,0:T(1,128)S(1)}, f32[1,32]{1,0:T(1,128)S(1)}, f32[1,32]{1,0:T(1,128)S(1)}) all-reduce(f32[1,32]{1,0:T(1,128)S(1)} %get-tuple-element.10, f32[1,32]{1,0:T(1,128)S(1)} %get-tuple-element.11, f32[1,32]{1,0:T(1,128)S(1)} %multiply_bitcast_fusion.2), channel_id=1, replica_groups=mesh['groups'=2,'row'=4,'col'=2,'rep'=2] {'row','col','rep'}, use_global_device_ids=true, to_apply=%region_11.0 | all-reduce | flops 96 | bytes 768 | tf_op jit(solution)/shard_map/psum | solution.py:28
  590.8 0.6 pad_maximum_fusion
  591.4 0.0 copy-done.1
  (2 shorter events, 0.0 us)
Async XLA Ops:
  7.2 102.8 %copy-start = (f32[32,4096]{1,0:T(8,128)S(1)}, f32[32,4096]{1,0:T(8,128)}, u32[]{:S(2)}) copy-start(f32[32,4096]{1,0:T(8,128)} %param.4) | copy-start | bytes 1572868
  7.2 102.8 %all-reduce.5.cloned.1.call-start = ((), (), s32[]{:S(2)}) async-start(), calls=%async_computation.3 | async-start | bytes 1048576 | tf_op jit(solution)/shard_map/psum | solution.py:21
  73.7 103.3 %copy-start.4 = (f32[32,4096]{1,0:T(8,128)S(1)}, f32[32,4096]{1,0:T(8,128)}, u32[]{:S(2)}) copy-start(f32[32,4096]{1,0:T(8,128)} %param.5) | copy-start | bytes 1572868
  73.7 103.3 %reduce-scatter.4.cloned.1.call-start = ((), (), s32[]{:S(2)}) async-start(), calls=%async_computation.4 | async-start | bytes 655360 | tf_op jit(solution)/shard_map/reduce_scatter | solution.py:25
  154.9 138.0 %all-reduce.7.cloned.1.call-start = ((), (), s32[]{:S(2)}) async-start(), calls=%async_computation.5 | async-start | bytes 1048576 | tf_op jit(solution)/shard_map/psum | solution.py:21
  260.9 99.1 %reduce-scatter.6.cloned.1.call-start = ((), (), s32[]{:S(2)}) async-start(), calls=%async_computation.6 | async-start | bytes 655360 | tf_op jit(solution)/shard_map/reduce_scatter | solution.py:25
  337.9 137.8 %all-reduce.9.cloned.1.call-start = ((), (), s32[]{:S(2)}) async-start(), calls=%async_computation.7 | async-start | bytes 1048576 | tf_op jit(solution)/shard_map/psum | solution.py:21
  443.6 100.4 %copy-start.2 = (f32[32,1024]{1,0:T(8,128)S(1)}, f32[32,1024]{1,0:T(8,128)}, u32[]{:S(2)}) copy-start(f32[32,1024]{1,0:T(8,128)} %reduce-scatter.4.cloned.1.call-done) | copy-start | bytes 393220
  443.6 100.4 %copy-start.3 = (f32[32,1024]{1,0:T(8,128)S(1)}, f32[32,1024]{1,0:T(8,128)}, u32[]{:S(2)}) copy-start(f32[32,1024]{1,0:T(8,128)} %reduce-scatter.6.cloned.1.call-done) | copy-start | bytes 393220
  443.6 100.3 %reduce-scatter.8.cloned.1.call-start = ((), (), s32[]{:S(2)}) async-start(), calls=%async_computation.8 | async-start | bytes 655360 | tf_op jit(solution)/shard_map/reduce_scatter | solution.py:25
  476.7 114.6 %copy-start.1 = (f32[32,4096]{1,0:T(8,128)}, f32[32,4096]{1,0:T(8,128)S(1)}, u32[]{:S(2)}) copy-start(f32[32,4096]{1,0:T(8,128)S(1)} %div.31) | copy-start | bytes 1572868
Sparse Core Ops, SparseCore 0:
  73.8 36.1 all-reduce.4
  155.0 21.9 reduce-scatter.3
  261.0 31.8 all-reduce.6
  338.0 21.9 reduce-scatter.5
  443.8 31.8 all-reduce.8
  522.0 21.9 reduce-scatter.7
